TPU v7x, 512 devices: a whole 4x4x16 slice. The times are simulated.
512 devices in a mesh: row: 16 (over z), col: 32 (over y, x, core).
Axes of the slice: x: 4, y: 4, z: 16, core: 2. Of those that a mesh axis runs over, the one named last changes fastest.
Arguments:
- tokens: bfloat16 [2048, 8192], P('row'), may hold values from -6 to 6
- gate_weight: bfloat16 [8192, 16384], P('row', 'col'), may hold values from -0.09375 to 0.09375
- up_weight: bfloat16 [8192, 16384], P('row', 'col'), may hold values from -0.09375 to 0.09375
- down_weight: bfloat16 [16384, 8192], P('col', 'row'), may hold values from -0.0625 to 0.0625
- gate_mask: int32 [64, 128], P('row', 'col'), may hold values from 0 to 1, as said below
- up_mask: int32 [64, 128], P('row', 'col'), may hold values from 0 to 1, as said below
- down_mask: int32 [128, 64], P('col', 'row'), may hold values 0 or 1
Outputs:
- mixed: bfloat16 [2048, 8192], P('col', 'row')
Inputs may be any that keep to these rules, and one draw needn't show every extreme that they name: `gate_mask`: each device's block of 4 x 4 tiles keeps between 4 and 12 tiles; in each column of devices some block keeps exactly 12. `up_mask`: as for gate_mask, drawn independently.
All inputs are finite; a program needn't handle non-finite values. No bound on the sum of `down_mask` on one device may be relied on, other than what follows from the above.
Results may differ from a plain program's by a relative error of at most 0.02.
Values may be sent and summed in bfloat16 or wider, within the bound.
A program may use at most 128 MiB of HBM per device.

v0:
```python
import jax
import jax.numpy as jnp
from jax import lax
from jax.sharding import PartitionSpec as P


def expand(weight, mask):
    rows, cols = weight.shape
    tile_rows, tile_cols = mask.shape
    tile = rows // tile_rows
    shaped = weight.reshape(tile_rows, tile, tile_cols, tile)
    return (shaped * mask.astype(weight.dtype)[:, None, :, None]).reshape(rows, cols)


def pack_tiles(weight, mask):
    rows, cols = weight.shape
    tile_rows, tile_cols = mask.shape
    tile = rows // tile_rows
    count = tile_rows * tile_cols
    slots = 3 * count // 4
    tiles = (
        weight.reshape(tile_rows, tile, tile_cols, tile)
        .transpose(0, 2, 1, 3)
        .reshape(count, tile * tile)
    )
    flags = mask.reshape(count)
    place = jnp.cumsum(flags) - 1
    chosen = (place[None, :] == jnp.arange(slots, dtype=jnp.int32)[:, None]) & (flags[None, :] == 1)
    packed = jnp.dot(chosen.astype(jnp.bfloat16), tiles, preferred_element_type=jnp.float32)
    packed = packed.astype(jnp.bfloat16).reshape(slots, tile, tile)
    where_from = jnp.sum(jnp.where(chosen, jnp.arange(count, dtype=jnp.int32)[None, :], 0), axis=1)
    return (packed, where_from)


def unpack_tiles(packed, where_from, groups, tile_rows, tile_cols):
    slots, tile = (packed.shape[0] // groups, packed.shape[1])
    count = tile_rows * tile_cols
    packed = packed.reshape(groups, slots, tile, tile)
    where_from = where_from.reshape(groups, slots)
    spread = (where_from[:, None, :] == jnp.arange(count, dtype=jnp.int32)[None, :, None]).astype(
        jnp.bfloat16
    )
    dense = jnp.einsum("gcs,gsab->gcab", spread, packed, preferred_element_type=jnp.float32).astype(
        jnp.bfloat16
    )
    dense = dense.reshape(groups, tile_rows, tile_cols, tile, tile).transpose(0, 1, 3, 2, 4)
    return dense.reshape(groups, tile_rows * tile, tile_cols * tile)


def on_device(tokens, gate_weight, up_weight, down_weight, gate_mask, up_mask, down_mask):
    tok_rows = tokens.shape[0]
    panel_rows, panel_cols = gate_weight.shape
    tile_rows, tile_cols = gate_mask.shape
    slots = 3 * tile_rows * tile_cols // 4
    gate_packed, gate_from = pack_tiles(gate_weight, gate_mask)
    up_packed, up_from = pack_tiles(up_weight, up_mask)
    gate_piece = lax.all_gather(gate_packed, "row", axis=0, tiled=True)
    up_piece = lax.all_gather(up_packed, "row", axis=0, tiled=True)
    gate_where = lax.all_gather(gate_from, "row", axis=0, tiled=True)
    up_where = lax.all_gather(up_from, "row", axis=0, tiled=True)
    groups = gate_piece.shape[0] // slots
    columns = tokens
    columns = columns.reshape(tok_rows, groups, panel_rows)

    def partial_value(piece, where_from):
        dense = unpack_tiles(piece, where_from, groups, tile_rows, tile_cols)
        product = jnp.einsum("tgr,grc->gtc", columns, dense, preferred_element_type=jnp.float32)
        rounded = lax.optimization_barrier(product.astype(jnp.bfloat16)).astype(jnp.float32)
        return jnp.sum(rounded, axis=0)

    gate = partial_value(gate_piece, gate_where)
    up = partial_value(up_piece, up_where)
    hidden = (jax.nn.silu(gate) * up).astype(jnp.bfloat16)
    all_hidden = lax.all_gather(hidden, "row", axis=0, tiled=True)
    down_eff = expand(down_weight, down_mask)
    return lax.psum_scatter(
        jnp.dot(all_hidden, down_eff, preferred_element_type=jnp.float32).astype(jnp.bfloat16),
        "col",
        scatter_dimension=0,
        tiled=True,
    )


def solution(mesh):
    return jax.shard_map(
        on_device,
        mesh=mesh,
        in_specs=(
            P("row", None),
            P("row", "col"),
            P("row", "col"),
            P("col", "row"),
            P("row", "col"),
            P("row", "col"),
            P("col", "row"),
        ),
        out_specs=P("col", "row"),
        check_vma=False,
    )
```

profile of v0, /device:TPU:2, one launch (start us, length us, event | category | flops | bytes accessed | tf_op | source)
XLA Modules:
  0.0 405.5 jit_solution(13095400725307765612)
XLA Ops:
  6.5 0.8 reshape.148
  7.3 0.7 broadcast_compare_fusion.1
  8.2 1.2 reshape.122
  10.0 0.8 slice
  10.9 0.8 reshape.149
  11.6 0.7 broadcast_compare_fusion
  12.4 1.2 reshape.130
  14.4 0.8 slice.1
  15.2 1.3 dynamic-slice
  17.9 26.8 %all-reduce.2 = (s32[192]{0:T(256)S(1)}, s32[192]{0:T(256)S(1)}) all-reduce(s32[192]{0:T(256)S(1)} %dynamic-update-slice.1, s32[192]{0:T(256)S(1)} %dynamic-update-slice), channel_id=1, replica_groups=mesh['row'=16,'col'=32] {'row'}, use_global_device_ids=true, to_apply=%add.1 | all-reduce | flops 384 | bytes 3072
  44.9 56.9 %all-gather.4.cloned.1.call-done = bf16[192,128,128]{2,1,0:T(8,128)(2,1)} async-done(((bf16[12,128,128]{2,1,0:T(8,128)(2,1)}), bf16[192,128,128]{2,1,0:T(8,128)(2,1)}) %all-gather.4.cloned.1.call-update) | async-done | bytes 6291472 | tf_op jit(solution)/shard_map/all_gather | solution.py:57
  101.7 10.4 %fusion.4 = bf16[16,16,128,128]{3,1,2,0:T(8,128)(2,1)} fusion(bf16[16,12,128,128]{3,2,1,0:T(8,128)(2,1)} %bitcast.65, s32[16,12]{1,0:T(8,128)S(1)} %eq.83), kind=kOutput, calls=%fused_computation.7 | convolution fusion | flops 104860672 | bytes 14680832 | tf_op jit(solution)/shard_map/gcs,gsab->gcab/dot_general | solution.py:43
  112.1 15.4 %copy.35 = bf16[16,4,128,4,128]{2,1,4,3,0:T(4,128)(2,1)} copy(bf16[16,4,128,4,128]{4,3,1,2,0:T(4,128)(2,1)} %bitcast.62) | data formatting | bytes 16777216 | tf_op jit(solution)/shard_map/transpose | solution.py:46
  127.6 13.2 %reshape.127 = bf16[16,512,512]{1,2,0:T(8,128)(2,1)} reshape(bf16[16,4,128,4,128]{2,1,4,3,0:T(4,128)(2,1)} %copy.35) | data formatting | bytes 16777216 | tf_op jit(solution)/shard_map/reshape | solution.py:47
  140.7 6.4 %convert_bitcast_fusion.1 = bf16[16,128,512]{1,2,0:T(8,128)(2,1)S(1)} fusion(bf16[16,512,512]{1,2,0:T(8,128)(2,1)} %reshape.127, bf16[16,16,8,512]{3,2,1,0:T(8,128)(2,1)} %bitcast.74), kind=kOutput, calls=%fused_computation.17 | convolution fusion | flops 1074790400 | bytes 12582912 | tf_op jit(solution)/shard_map/tgr,grc->gtc/dot_general | solution.py:67
  147.2 39.8 %all-gather.6.cloned.1.call-done = bf16[192,128,128]{2,1,0:T(8,128)(2,1)} async-done(((bf16[12,128,128]{2,1,0:T(8,128)(2,1)}), bf16[192,128,128]{2,1,0:T(8,128)(2,1)}) %all-gather.6.cloned.1.call-update) | async-done | bytes 6291472 | tf_op jit(solution)/shard_map/all_gather | solution.py:58
  186.9 7.2 %fusion.7 = bf16[16,16,128,128]{3,1,2,0:T(8,128)(2,1)S(1)} fusion(bf16[16,12,128,128]{3,2,1,0:T(8,128)(2,1)} %bitcast.66, s32[16,12]{1,0:T(8,128)S(1)} %eq.92), kind=kOutput, calls=%fused_computation.8 | convolution fusion | flops 104860672 | bytes 14680832 | tf_op jit(solution)/shard_map/gcs,gsab->gcab/dot_general | solution.py:43
  194.1 5.8 %copy.81 = bf16[16,4,4,128,128]{4,2,3,1,0:T(4,128)(2,1)} copy(bf16[16,4,4,128,128]{4,2,1,3,0:T(4,128)(2,1)S(1)} %bitcast.63) | data formatting | bytes 16777216 | tf_op jit(solution)/shard_map/reshape | solution.py:46
  200.0 13.1 %reshape.135 = bf16[16,512,512]{2,1,0:T(8,128)(2,1)} reshape(bf16[16,4,128,4,128]{4,3,2,1,0:T(4,128)(2,1)} %bitcast.64) | data formatting | bytes 16777216 | tf_op jit(solution)/shard_map/reshape | solution.py:47
  213.1 6.6 %convert_bitcast_fusion = bf16[16,128,512]{1,2,0:T(8,128)(2,1)S(1)} fusion(bf16[16,512,512]{2,1,0:T(8,128)(2,1)} %reshape.135, bf16[16,16,8,512]{3,2,1,0:T(8,128)(2,1)} %bitcast.75), kind=kOutput, calls=%fused_computation.16 | convolution fusion | flops 1074790400 | bytes 12582912 | tf_op jit(solution)/shard_map/tgr,grc->gtc/dot_general | solution.py:67
  220.2 0.7 multiply_convert_fusion
  221.0 75.3 %all-gather.8.cloned.1.call-done = bf16[2048,512]{0,1:T(8,128)(2,1)} async-done(((bf16[128,512]{0,1:T(8,128)(2,1)}), bf16[2048,512]{0,1:T(8,128)(2,1)}) %all-gather.8.cloned.1.call-update) | async-done | bytes 2097168 | tf_op jit(solution)/shard_map/all_gather | solution.py:74
  296.6 4.2 %convolution_convert_fusion.2 = bf16[2048,512]{1,0:T(8,128)(2,1)} fusion(bf16[2048,512]{0,1:T(8,128)(2,1)} %all-gather.8.cloned.1.call-done, bf16[512,512]{1,0:T(8,128)(2,1)S(1)} %copy-done.1, bf16[64,8,4,128]{3,2,1,0:T(4,128)(2,1)S(1)} %bitcast.73), kind=kOutput, calls=%fused_computation.11 | convolution fusion | flops 1075052544 | bytes 5242880 | tf_op jit(solution)/shard_map/dot_general | solution.py:77
  300.8 98.1 %reduce-scatter.2.cloned.1.call-done = bf16[64,512]{1,0:T(8,128)(2,1)} async-done(((bf16[2048,512]{1,0:T(8,128)(2,1)}), bf16[64,512]{1,0:T(8,128)(2,1)}) %reduce-scatter.2.cloned.1.call-update) | async-done | bytes 65552 | tf_op jit(solution)/shard_map/reduce_scatter | solution.py:76
  (35 shorter events, 3.5 us)
Async XLA Ops:
  6.5 95.2 %all-gather.4.cloned.1.call-start = ((), (), s32[]{:S(2)}) async-start(), calls=%async_computation.1 | async-start | bytes 6684672 | tf_op jit(solution)/shard_map/all_gather | solution.py:57
  10.8 176.1 %all-gather.6.cloned.1.call-start = ((), (), s32[]{:S(2)}) async-start(), calls=%async_computation.2 | async-start | bytes 6684672 | tf_op jit(solution)/shard_map/all_gather | solution.py:58
  15.2 281.1 %all-gather.8.cloned.1.call-start = ((), (), s32[]{:S(2)}) async-start(), calls=%async_computation.3 | async-start | bytes 2228224 | tf_op jit(solution)/shard_map/all_gather | solution.py:74
  213.1 7.9 %copy-start = (s32[4,4]{1,0:T(4,128)S(1)}, s32[4,4]{1,0:T(4,128)}, u32[]{:S(2)}) copy-start(s32[4,4]{1,0:T(4,128)} %param.13) | copy-start | bytes 196
  213.1 83.5 %copy-start.1 = (bf16[512,512]{1,0:T(8,128)(2,1)S(1)}, bf16[512,512]{1,0:T(8,128)(2,1)}, u32[]{:S(2)}) copy-start(bf16[512,512]{1,0:T(8,128)(2,1)} %param.10) | copy-start | bytes 1572868
  220.9 178.0 %reduce-scatter.2.cloned.1.call-start = ((), (), s32[]{:S(2)}) async-start(), calls=%async_computation.4 | async-start | bytes 2162688 | tf_op jit(solution)/shard_map/reduce_scatter | solution.py:76
Sparse Core Ops, SparseCore 0:
  11.0 90.7 all-gather.3
  103.8 83.0 all-gather.5
  221.1 75.2 all-gather.7
  300.9 97.9 reduce-scatter.1
where the time goes:
time: 407 us; the launch traced here: 405 us
  waiting for transfers between devices  270 us (66%)
  local copies, waits for them, and re-layouts  55.7 us (14%)
  matrix products  35.5 us (9%)
  blocking collectives  26.8 us (7%)
  between operations  13.9 us (3%)
    reduce_scatter x1, waiting for transfers between devices, on_device(): lax.psum_scatter(jnp.dot(all_hidden, down_eff, preferred_element_type=jnp...  98.1 us
    all_gather x1, waiting for transfers between devices, on_device(): all_hidden = lax.all_gather(hidden, 'row', axis=0, tiled=True)  75.3 us
    all_gather x1, waiting for transfers between devices, on_device(): gate_piece = lax.all_gather(gate_packed, 'row', axis=0, tiled=True)  56.9 us
    all_gather x1, waiting for transfers between devices, on_device(): up_piece = lax.all_gather(up_packed, 'row', axis=0, tiled=True)  39.8 us
    unnamed x1, blocking collectives  26.8 us
    reshape x2, local copies, waits for them, and re-layouts, unpack_tiles(): return dense.reshape(groups, tile_rows * tile, tile_cols * tile)  26.3 us
    dot_general x2, matrix products, unpack_tiles(): jnp.einsum('gcs,gsab->gcab', spread, packed, preferred_element_type=jnp.f...  17.6 us
    transpose x1, local copies, waits for them, and re-layouts, unpack_tiles(): dense.reshape(groups, tile_rows, tile_cols, tile, tile)  15.4 us
  transfers between devices with their start and end apart: 4, of which 4 were waited for; matrix products, arithmetic and copies ran while one was open for 13% of the time, Pallas kernels for 0%

commit v1 on v0

--- a/solution.py
+++ b/solution.py
@@ -54,7 +54,9 @@
     slots = 3 * tile_rows * tile_cols // 4
     gate_packed, gate_from = pack_tiles(gate_weight, gate_mask)
     up_packed, up_from = pack_tiles(up_weight, up_mask)
-    gate_piece = lax.all_gather(gate_packed, "row", axis=0, tiled=True)
+    gate_piece = jnp.concatenate(
+        lax.all_to_all(jnp.stack([gate_packed] * lax.axis_size("row")), "row", 0, 0), axis=0
+    )
     up_piece = lax.all_gather(up_packed, "row", axis=0, tiled=True)
     gate_where = lax.all_gather(gate_from, "row", axis=0, tiled=True)
     up_where = lax.all_gather(up_from, "row", axis=0, tiled=True)

time: 407 us -> 644 us (1.58)
  blocking collectives: 26.8 us -> 342 us
  waiting for transfers between devices: 270 us -> 176 us
  starting transfers between devices: 0.13 us -> 15.5 us
    unnamed x1, blocking collectives: 26.8 us -> 342 us
    all_gather x1 -> x0, waiting for transfers between devices: 56.9 us -> none  [on_device(): gate_piece = lax.all_gather(gate_packed, 'row', axis=0, tiled=True)]
    all_gather x1, waiting for transfers between devices: 39.8 us -> 0.02 us  [on_device(): up_piece = lax.all_gather(up_packed, 'row', axis=0, tiled=True)]
    all_to_all x0 -> x1, starting transfers between devices: none -> 15.4 us  [on_device(): lax.all_to_all(jnp.stack([gate_packed] * lax.axis_size('row')), 'row', 0, 0)]
  transfers between devices with their start and end apart: 4 -> 4, of which waited for: 4 -> 2; matrix products, arithmetic and copies ran while one was open for 13% -> 6% of each run, Pallas kernels for 0% -> 0%
where the time goes in v1:
time: 644 us; the launch traced here: 642 us
  blocking collectives  342 us (53%)
  waiting for transfers between devices  176 us (27%)
  local copies, waits for them, and re-layouts  57.4 us (9%)
  matrix products  35.4 us (5%)
  starting transfers between devices  15.5 us (2%)
  between operations  13.9 us (2%)
    unnamed x1, blocking collectives  342 us
    reduce_scatter x1, waiting for transfers between devices, on_device(): lax.psum_scatter(jnp.dot(all_hidden, down_eff, preferred_element_type=jnp...  98.1 us
    all_gather x1, waiting for transfers between devices, on_device(): all_hidden = lax.all_gather(hidden, 'row', axis=0, tiled=True)  77.3 us
    reshape x2, local copies, waits for them, and re-layouts, unpack_tiles(): return dense.reshape(groups, tile_rows * tile, tile_cols * tile)  26.2 us
    dot_general x2, matrix products, unpack_tiles(): jnp.einsum('gcs,gsab->gcab', spread, packed, preferred_element_type=jnp.f...  17.6 us
    all_to_all x1, starting transfers between devices, on_device(): lax.all_to_all(jnp.stack([gate_packed] * lax.axis_size('row')), 'row', 0, 0)  15.4 us
    transpose x1, local copies, waits for them, and re-layouts, unpack_tiles(): dense.reshape(groups, tile_rows, tile_cols, tile, tile)  15.3 us
  transfers between devices with their start and end apart: 4, of which 2 were waited for; matrix products, arithmetic and copies ran while one was open for 6% of the time, Pallas kernels for 0%

profile of v1, /device:TPU:2, one launch (start us, length us, event | category | flops | bytes accessed | tf_op | source)
XLA Modules:
  0.0 642.5 jit_solution(8966633429543696483)
XLA Ops:
  6.5 0.8 reshape.142
  7.3 0.7 broadcast_compare_fusion.1
  8.2 1.2 reshape.118
  9.5 0.4 convolution_convert_fusion.1
  10.0 4.2 stack.3
  14.3 15.4 %all-to-all-start = ((bf16[16,12,128,128]{3,2,1,0:T(8,128)(2,1)}), bf16[16,12,128,128]{3,2,1,0:T(8,128)(2,1)}, u32[]{:S(2)}, u32[]{:S(2)}) async-start(bf16[16,12,128,128]{3,2,1,0:T(8,128)(2,1)} %stack.3), calls=%async_computation | async-start | bytes 12582912 | tf_op jit(solution)/shard_map/all_to_all | solution.py:58
  30.3 0.4 convolution_convert_fusion
  30.8 0.8 slice.1
  31.7 1.3 dynamic-slice
  33.7 0.2 dynamic-update-slice
  34.3 342.1 %all-reduce.2 = (s32[192]{0:T(256)S(1)}, s32[192]{0:T(256)S(1)}) all-reduce(s32[192]{0:T(256)S(1)} %dynamic-update-slice.1, s32[192]{0:T(256)S(1)} %dynamic-update-slice), channel_id=1, replica_groups=mesh['row'=16,'col'=32] {'row'}, use_global_device_ids=true, to_apply=%add.1 | all-reduce | flops 384 | bytes 3072
  376.6 7.2 %fusion.7 = bf16[16,16,128,128]{3,1,2,0:T(8,128)(2,1)S(1)} fusion(bf16[16,12,128,128]{3,2,1,0:T(8,128)(2,1)} %bitcast.64, s32[16,12]{1,0:T(8,128)S(1)} %eq.92), kind=kOutput, calls=%fused_computation.8 | convolution fusion | flops 104860672 | bytes 14680832 | tf_op jit(solution)/shard_map/gcs,gsab->gcab/dot_general | solution.py:43
  383.8 6.0 copy.82
  389.8 13.1 %reshape.129 = bf16[16,512,512]{2,1,0:T(8,128)(2,1)} reshape(bf16[16,4,128,4,128]{4,3,2,1,0:T(4,128)(2,1)} %bitcast.63) | data formatting | bytes 16777216 | tf_op jit(solution)/shard_map/reshape | solution.py:47
  402.9 6.5 %convert_bitcast_fusion = bf16[16,128,512]{1,2,0:T(8,128)(2,1)S(1)} fusion(bf16[16,512,512]{2,1,0:T(8,128)(2,1)} %reshape.129, bf16[16,16,8,512]{3,2,1,0:T(8,128)(2,1)} %bitcast.72), kind=kOutput, calls=%fused_computation.16 | convolution fusion | flops 1074790400 | bytes 12582912 | tf_op jit(solution)/shard_map/tgr,grc->gtc/dot_general | solution.py:69
  409.4 10.4 %fusion.4 = bf16[16,16,128,128]{3,1,2,0:T(8,128)(2,1)} fusion(bf16[16,12,128,128]{3,2,1,0:T(8,128)(2,1)} %all-to-all-done, s32[16,12]{1,0:T(8,128)S(1)} %eq.83), kind=kOutput, calls=%fused_computation.7 | convolution fusion | flops 104860672 | bytes 14680832 | tf_op jit(solution)/shard_map/gcs,gsab->gcab/dot_general | solution.py:43
  419.8 15.3 %copy.36 = bf16[16,4,128,4,128]{2,1,4,3,0:T(4,128)(2,1)} copy(bf16[16,4,128,4,128]{4,3,1,2,0:T(4,128)(2,1)} %bitcast.62) | data formatting | bytes 16777216 | tf_op jit(solution)/shard_map/transpose | solution.py:46
  435.1 13.1 %reshape.121 = bf16[16,512,512]{1,2,0:T(8,128)(2,1)} reshape(bf16[16,4,128,4,128]{2,1,4,3,0:T(4,128)(2,1)} %copy.36) | data formatting | bytes 16777216 | tf_op jit(solution)/shard_map/reshape | solution.py:47
  448.2 6.4 convert_bitcast_fusion.1
  454.6 0.6 convert_reduce_fusion
  455.2 0.7 multiply_convert_fusion
  456.0 77.3 %all-gather.5.cloned.1.call-done = bf16[2048,512]{0,1:T(8,128)(2,1)} async-done(((bf16[128,512]{0,1:T(8,128)(2,1)}), bf16[2048,512]{0,1:T(8,128)(2,1)}) %all-gather.5.cloned.1.call-update) | async-done | bytes 2097168 | tf_op jit(solution)/shard_map/all_gather | solution.py:76
  533.6 4.2 convolution_convert_fusion.2
  537.8 98.1 %reduce-scatter.2.cloned.1.call-done = bf16[64,512]{1,0:T(8,128)(2,1)} async-done(((bf16[2048,512]{1,0:T(8,128)(2,1)}), bf16[64,512]{1,0:T(8,128)(2,1)}) %reduce-scatter.2.cloned.1.call-update) | async-done | bytes 65552 | tf_op jit(solution)/shard_map/reduce_scatter | solution.py:78
  (39 shorter events, 2.1 us)
Async XLA Ops:
  14.3 15.4 %copy-start.1 = (s32[4,4]{1,0:T(4,128)S(1)}, s32[4,4]{1,0:T(4,128)}, u32[]{:S(2)}) copy-start(s32[4,4]{1,0:T(4,128)} %param.12) | copy-start | bytes 196
  14.3 15.6 %copy-start = (bf16[512,512]{1,0:T(8,128)(2,1)S(1)}, bf16[512,512]{1,0:T(8,128)(2,1)}, u32[]{:S(2)}) copy-start(bf16[512,512]{1,0:T(8,128)(2,1)} %param.9) | copy-start | bytes 1572868
  14.3 395.1 %all-to-all-start = ((bf16[16,12,128,128]{3,2,1,0:T(8,128)(2,1)}), bf16[16,12,128,128]{3,2,1,0:T(8,128)(2,1)}, u32[]{:S(2)}, u32[]{:S(2)}) async-start(bf16[16,12,128,128]{3,2,1,0:T(8,128)(2,1)} %stack.3), calls=%async_computation | async-start | bytes 12582912 | tf_op jit(solution)/shard_map/all_to_all | solution.py:58
  29.7 346.9 %all-gather.3.cloned.1.call-start = ((), (), s32[]{:S(2)}) async-start(), calls=%async_computation.2 | async-start | bytes 6684672 | tf_op jit(solution)/shard_map/all_gather | solution.py:60
  31.6 501.7 %all-gather.5.cloned.1.call-start = ((), (), s32[]{:S(2)}) async-start(), calls=%async_computation.3 | async-start | bytes 2228224 | tf_op jit(solution)/shard_map/all_gather | solution.py:76
  448.2 7.8 %copy-start.2 = (s32[4,4]{1,0:T(4,128)S(1)}, s32[4,4]{1,0:T(4,128)}, u32[]{:S(2)}) copy-start(s32[4,4]{1,0:T(4,128)} %param.13) | copy-start | bytes 196
  448.2 85.3 %copy-start.3 = (bf16[512,512]{1,0:T(8,128)(2,1)S(1)}, bf16[512,512]{1,0:T(8,128)(2,1)}, u32[]{:S(2)}) copy-start(bf16[512,512]{1,0:T(8,128)(2,1)} %param.10) | copy-start | bytes 1572868
  455.9 180.0 %reduce-scatter.2.cloned.1.call-start = ((), (), s32[]{:S(2)}) async-start(), calls=%async_computation.4 | async-start | bytes 2162688 | tf_op jit(solution)/shard_map/reduce_scatter | solution.py:78
Sparse Core Ops, SparseCore 0:
  32.6 334.4 all-gather.2
  456.1 77.2 all-gather.4
  537.9 97.9 reduce-scatter.1
